TPU v7x, 256 devices: a whole 4x4x8 slice. The times are simulated.
256 devices in a mesh: shell: 128 (over x, y, z), radial: 2 (over core).
Axes of the slice: x: 4, y: 4, z: 8, core: 2. Of those that a mesh axis runs over, the one named last changes fastest.
Arguments:
- state: float32 [8, 32, 1024, 128], P(None, 'radial', 'shell')
- footpoints: int32 [32, 1024, 128], P('radial', 'shell'), may hold values from 0 to 32767, as said below
- conductance: float32 [4, 128, 256], P(None, 'shell', 'radial'), may hold values from 0.1 to 0.45
- inverse_blocks: float32 [128, 2, 128, 128], P('shell', 'radial')
Outputs:
- state_next: float32 [8, 32, 1024, 128], P(None, 'radial', 'shell')
- potential: float32 [128, 256], P('shell', 'radial')
- footpoint_potential: float32 [32, 1024, 128], P('radial', 'shell')
Inputs may be any that keep to these rules, and one draw needn't show every extreme that they name: `footpoints`: A cell whose longitude index lon lies in shell block s = lon // 8 maps to a node whose column (node % 256) lies in s * 2 to (s + 1) * 2 - 1.
All inputs are finite; a program needn't handle non-finite values.
Results may differ from a plain program's by a relative error of at most 0.0003.
Values sent between devices are 32-bit elements; how exact they have to be, the bound alone decides.
A program may use at most 64 MiB of HBM per device.

v0:
```python
import jax
import jax.numpy as jnp
from jax import lax
from jax.sharding import PartitionSpec as P

NLAT_I = 128
NLON_I = 256
ITERS_I = 4
GAMMA = 5.0 / 3.0
TIME_STEP = 0.02
CELL_AREA = 0.125


def padded_2(block, sides, width, periodic):
    for axis, dim in sides:
        count = lax.axis_size(axis)
        forward = [(i, i + 1) for i in range(count - 1)]
        if periodic:
            forward.append((count - 1, 0))
        backward = [(target, source) for source, target in forward]
        low = lax.ppermute(
            lax.slice_in_dim(block, block.shape[dim] - width, None, axis=dim), axis, forward
        )
        high = lax.ppermute(lax.slice_in_dim(block, 0, width, axis=dim), axis, backward)
        block = jnp.concatenate([low, block, high], axis=dim)
    return block


def minmod(first_jump, second_jump):
    return (
        0.5
        * (jnp.sign(first_jump) + jnp.sign(second_jump))
        * jnp.minimum(jnp.abs(first_jump), jnp.abs(second_jump))
    )


def physical_flux(conserved, direction):
    density = conserved[0]
    velocity = conserved[1:4] / density
    magnetic = conserved[4:7]
    energy = conserved[7]
    field_sq = jnp.sum(magnetic * magnetic, axis=0)
    kinetic = jnp.sum(velocity * velocity, axis=0)
    pressure = (GAMMA - 1.0) * (energy - 0.5 * density * kinetic - 0.5 * field_sq)
    total_pressure = pressure + 0.5 * field_sq
    normal_speed = velocity[direction]
    normal_field = magnetic[direction]
    selector = (jnp.arange(3) == direction).astype(jnp.float32).reshape((3,) + (1,) * density.ndim)
    momentum_flux = (
        density * velocity * normal_speed - magnetic * normal_field + total_pressure * selector
    )
    induction = normal_speed * magnetic - normal_field * velocity
    alignment = jnp.sum(velocity * magnetic, axis=0)
    energy_flux = (energy + total_pressure) * normal_speed - normal_field * alignment
    fluxes = jnp.concatenate(
        [(density * normal_speed)[None], momentum_flux, induction, energy_flux[None]], axis=0
    )
    signal = jnp.abs(normal_speed) + jnp.sqrt((GAMMA * jnp.abs(pressure) + field_sq) / density)
    return (fluxes, signal)


def face_divergence(padded, direction):
    dimension = direction + 1
    cell_count = padded.shape[dimension] - 4

    def window_slice(array, first_index, length):
        return lax.slice_in_dim(array, first_index, first_index + length, axis=dimension)

    jumps = window_slice(padded, 1, cell_count + 3) - window_slice(padded, 0, cell_count + 3)
    slopes = minmod(window_slice(jumps, 1, cell_count + 2), window_slice(jumps, 0, cell_count + 2))
    left_state = window_slice(padded, 1, cell_count + 1) + 0.5 * window_slice(
        slopes, 0, cell_count + 1
    )
    right_state = window_slice(padded, 2, cell_count + 1) - 0.5 * window_slice(
        slopes, 1, cell_count + 1
    )
    left_flux, left_signal = physical_flux(left_state, direction)
    right_flux, right_signal = physical_flux(right_state, direction)
    signal_max = jnp.maximum(left_signal, right_signal)
    face_flux = 0.5 * (left_flux + right_flux) - 0.5 * signal_max * (right_state - left_state)
    return window_slice(face_flux, 1, cell_count) - window_slice(face_flux, 0, cell_count)


def tendency(padded):
    total_div = face_divergence(padded[:, :, 2:-2, 2:-2], 0)
    total_div = total_div + face_divergence(padded[:, 2:-2, :, 2:-2], 1)
    total_div = total_div + face_divergence(padded[:, 2:-2, 2:-2, :], 2)
    return -total_div


def shifted(values, direction, offset):
    for dimension in range(3):
        first_index = offset if dimension == direction else 2
        length = values.shape[dimension] - 4
        values = lax.slice_in_dim(values, first_index, first_index + length, axis=dimension)
    return values


def field_current(padded):
    magnetic = padded[4:7]

    def derivative(component, direction):
        return 0.5 * (
            shifted(magnetic[component], direction, 3) - shifted(magnetic[component], direction, 1)
        )

    curl_first = derivative(2, 1) - derivative(1, 2)
    curl_second = derivative(0, 2) - derivative(2, 0)
    curl_third = derivative(1, 0) - derivative(0, 1)
    centre = [shifted(magnetic[component], 0, 2) for component in range(3)]
    field_sq = centre[0] * centre[0] + centre[1] * centre[1] + centre[2] * centre[2]
    aligned = curl_first * centre[0] + curl_second * centre[1] + curl_third * centre[2]
    return CELL_AREA * aligned / jnp.sqrt(1.0 + field_sq)


def pad_latitude(field):
    return jnp.pad(field, ((0, 0), (0, 0), (0, 0), (2, 2)), mode="edge")


def fill_radial(field, margin):
    position = lax.axis_index("radial")
    last_index = lax.axis_size("radial") - 1
    extent = field.shape[1]
    layer_index = lax.broadcasted_iota(jnp.int32, (1, extent, 1, 1), 1)
    lower_edge = lax.slice_in_dim(field, margin, margin + 1, axis=1)
    upper_edge = lax.slice_in_dim(field, extent - margin - 1, extent - margin, axis=1)
    field = jnp.where((layer_index < margin) & (position == 0), lower_edge, field)
    return jnp.where((layer_index >= extent - margin) & (position == last_index), upper_edge, field)


def extended_cells(field):
    grown = padded_2(field, (("shell", 2), ("radial", 1)), 2, True)
    return pad_latitude(fill_radial(grown, 2))


def body(state, footpoints, conductance, inverse_blocks):
    first_padded = extended_cells(state)
    section_one = state + TIME_STEP * tendency(first_padded)
    second_padded = extended_cells(section_one)
    state_next = 0.5 * state + 0.5 * (section_one + TIME_STEP * tendency(second_padded))
    cell_current = field_current(first_padded).reshape(-1)
    rows_owned = inverse_blocks.shape[0]
    half_width = inverse_blocks.shape[2]
    halves_count = lax.axis_size("radial")
    latitude_node = footpoints // NLON_I
    column_node = footpoints % NLON_I
    owner_index = latitude_node // rows_owned * halves_count + column_node // half_width
    node_slot = (
        owner_index * (rows_owned * half_width)
        + latitude_node % rows_owned * half_width
        + column_node % half_width
    )
    partial_sums = jax.ops.segment_sum(
        cell_current, node_slot.reshape(-1), num_segments=NLAT_I * NLON_I
    )
    currents = lax.psum_scatter(
        partial_sums, ("shell", "radial"), scatter_dimension=0, tiled=True
    ).reshape(rows_owned, half_width)
    block_matrices = inverse_blocks[:, 0]

    def apply_blocks(vector):
        return jnp.einsum("rij,rj->ri", block_matrices, vector, precision=lax.Precision.HIGHEST)

    potential = apply_blocks(currents)
    for sweep_index in range(ITERS_I - 1):
        padded_panel = padded_2(potential, (("shell", 0), ("radial", 1)), 1, False)
        coupled = currents + conductance[0] * padded_panel[:-2, 1:-1]
        coupled = coupled + conductance[1] * padded_panel[2:, 1:-1]
        coupled = coupled + conductance[2] * padded_panel[1:-1, :-2]
        coupled = coupled + conductance[3] * padded_panel[1:-1, 2:]
        potential = apply_blocks(coupled)
    whole_table = lax.all_gather(potential.reshape(-1), ("shell", "radial"), axis=0, tiled=True)
    footpoint_potential = whole_table[node_slot]
    return (state_next, potential, footpoint_potential)


def solution(mesh):
    return jax.shard_map(
        body,
        mesh=mesh,
        in_specs=(
            P(None, "radial", "shell", None),
            P("radial", "shell", None),
            P(None, "shell", "radial"),
            P("shell", "radial", None, None),
        ),
        out_specs=(
            P(None, "radial", "shell", None),
            P("shell", "radial"),
            P("radial", "shell", None),
        ),
        check_vma=False,
    )
```

profile of v0, /device:TPU:1, one launch (start us, length us, event | category | flops | bytes accessed | tf_op | source)
XLA Modules:
  0.0 684.3 jit_solution(17312191880690666836)
XLA Ops:
  7.2 1.4 fusion.271
  8.6 2.5 collective-permute-start
  11.1 8.7 %collective-permute-start.1 = (f32[8,16,2,128]{3,2,1,0:T(2,128)S(1)}, f32[8,16,2,128]{3,2,1,0:T(2,128)S(1)}, u32[]{:S(2)}, u32[]{:S(2)}) collective-permute-start(f32[8,16,2,128]{3,2,1,0:T(2,128)S(1)} %get-tuple-element.179), channel_id=1, source_target_pairs={{2,0},{4,2},{6,4},{8,6},{10,8},{12,10},{14,12},{16,14},{18,16},{20... | collective-permute-start | bytes 393224 | tf_op jit(solution)/shard_map/ppermute | solution.py:24
  20.9 1.6 fusion.158
  23.2 0.9 pad_maximum_fusion.19
  24.1 1.1 collective-permute-start.2
  26.9 0.9 slice_subtract_fusion.4
  27.8 1.1 slice_subtract_fusion.2
  28.9 1.6 fusion.269
  30.5 2.5 copy.843
  33.0 1.2 copy.844
  36.1 2.6 pad_maximum_fusion
  39.9 1.5 multiply_reduce_fusion.31
  42.6 1.8 multiply_reduce_fusion.22
  45.0 1.6 multiply_reduce_fusion.19
  49.1 86.9 %scatter_custom_fusion = f32[32768]{0:T(1024)} fusion(s32[16384]{0:T(1024)} %bitcast.618, f32[16384]{0:T(1024)} %bitcast.619, f32[]{:T(128)} %constant.97.clone.1), kind=kCustom, calls=%fused_computation.431 | custom fusion | flops 16384 | bytes 131584 | tf_op jit(solution)/shard_map/scatter-add | solution.py:153
  136.0 2.6 slice_subtract_fusion.1
  147.7 1.3 fusion.14
  149.0 0.9 multiply_add_fusion.10
  149.9 228.3 %all-reduce.3.cloned.1.call-done = f32[32768]{0:T(1024)} async-done(((f32[32768]{0:T(1024)}), f32[32768]{0:T(1024)}) %all-reduce.3.cloned.1.call-update) | async-done | bytes 131088
  379.1 1.3 collective-permute-start.9
  380.5 4.4 collective-permute-start.8
  384.9 1.4 fusion.24
  386.4 1.3 collective-permute-start.10
  387.7 4.2 collective-permute-start.11
  392.9 1.5 collective-permute-start.13
  394.3 4.3 collective-permute-start.12
  399.5 1.3 collective-permute-start.14
  400.8 3.1 collective-permute-start.15
  404.9 1.3 collective-permute-start.17
  406.2 4.5 collective-permute-start.16
  410.9 1.8 collective-permute-start.4
  412.7 5.2 collective-permute-start.5
  417.9 1.3 collective-permute-start.18
  419.2 3.1 collective-permute-start.19
  423.4 61.8 %all-gather = f32[256,1,128]{2,1,0:T(1,128)S(1)} all-gather(f32[1,1,128]{2,1,0:T(1,128)S(1)} %bitcast.621), channel_id=1, replica_groups=mesh['shell'=128,'radial'=2] {'shell','radial'}, dimensions={0}, use_global_device_ids=true | all-gather | bytes 131584 | tf_op jit(solution)/shard_map/all_gather | solution.py:172
  485.1 160.6 %gather_fusion = f32[16384]{0:T(1024)} fusion(f32[32768]{0:T(1024)S(1)} %bitcast.598, s32[16384]{0:T(1024)S(1)} %copy-done.67), kind=kCustom, calls=%fused_computation | custom fusion | bytes 196608 | tf_op jit(solution)/shard_map/gather | solution.py:173
  646.4 0.8 collective-permute-done.6
  648.2 1.9 fusion.268
  650.5 1.4 multiply_reduce_fusion.28
  652.0 1.4 multiply_reduce_fusion.25
  654.6 1.8 multiply_reduce_fusion.10
  657.0 1.6 multiply_reduce_fusion.7
  659.3 3.2 copy.860
  662.5 3.2 copy.861
  665.7 1.3 reshape.264
  667.4 1.0 fusion.4
  676.4 1.1 fusion.32
  (276 shorter events, 37.0 us)
Async XLA Ops:
  7.2 371.8 %copy-start = (f32[1,1,128,128]{3,2,1,0:T(8,128)S(1)}, f32[1,1,128,128]{3,2,1,0:T(8,128)}, u32[]{:S(2)}) copy-start(f32[1,1,128,128]{3,2,1,0:T(8,128)} %param.7) | copy-start | bytes 196612
  7.2 18.3 %copy-start.4 = (f32[8,16,8,128]{3,2,1,0:T(8,128)S(1)}, f32[8,16,8,128]{3,2,1,0:T(8,128)}, u32[]{:S(2)}) copy-start(f32[8,16,8,128]{3,2,1,0:T(8,128)} %param.4) | copy-start | bytes 1572868
  7.2 371.0 %all-reduce.3.cloned.1.call-start = ((), (), s32[]{:S(2)}) async-start(), calls=%async_computation | async-start | bytes 262144
  8.6 14.5 %collective-permute-start = (f32[8,16,2,128]{3,2,1,0:T(2,128)S(1)}, f32[8,16,2,128]{3,2,1,0:T(2,128)S(1)}, u32[]{:S(2)}, u32[]{:S(2)}) collective-permute-start(f32[8,16,2,128]{3,2,1,0:T(2,128)S(1)} %get-tuple-element.178), channel_id=1, source_target_pairs={{0,2},{2,4},{4,6},{6,8},{8,10},{10,12},{12,14},{14,16},{16,18},{18... | collective-permute-start | bytes 393224 | tf_op jit(solution)/shard_map/ppermute | solution.py:21
  11.1 12.0 %collective-permute-start.1 = (f32[8,16,2,128]{3,2,1,0:T(2,128)S(1)}, f32[8,16,2,128]{3,2,1,0:T(2,128)S(1)}, u32[]{:S(2)}, u32[]{:S(2)}) collective-permute-start(f32[8,16,2,128]{3,2,1,0:T(2,128)S(1)} %get-tuple-element.179), channel_id=1, source_target_pairs={{2,0},{4,2},{6,4},{8,6},{10,8},{12,10},{14,12},{16,14},{18,16},{20... | collective-permute-start | bytes 393224 | tf_op jit(solution)/shard_map/ppermute | solution.py:24
  23.1 3.8 copy-start.68
  24.1 2.1 collective-permute-start.2
  25.2 1.3 collective-permute-start.3
  36.1 2.6 copy-start.18
  39.1 2.3 copy-start.14
  39.1 2.3 copy-start.13
  42.5 4.1 copy-start.9
  42.5 4.1 copy-start.11
  42.6 4.1 copy-start.27
  140.9 2.6 copy-start.59
  140.9 3.2 copy-start.21
  140.9 3.2 copy-start.34
  140.9 3.2 copy-start.50
  141.0 3.2 copy-start.52
  141.1 3.1 copy-start.10
  141.1 3.1 copy-start.12
  141.1 3.1 copy-start.20
  141.1 3.1 copy-start.33
  149.0 235.9 %copy-start.58 = (f32[17,8,128]{2,1,0:T(8,128)S(1)}, f32[17,8,128]{2,1,0:T(8,128)}, u32[]{:S(2)}) copy-start(f32[17,8,128]{2,1,0:T(8,128)} %get-tuple-element.83) | copy-start | bytes 208900
  379.1 7.2 %collective-permute-start.9 = (f32[1,128]{1,0:T(1,128)S(1)}, f32[1,128]{1,0:T(1,128)S(1)}, u32[]{:S(2)}, u32[]{:S(2)}) collective-permute-start(f32[1,128]{1,0:T(1,128)S(1)} %fusion.181), channel_id=1, source_target_pairs={{2,0},{4,2},{6,4},{8,6},{10,8},{12,10},{14,12},{16,14},{18,16},{20... | collective-permute-start | bytes 1544 | tf_op jit(solution)/shard_map/ppermute | solution.py:24
  380.5 5.9 collective-permute-start.8
  384.9 7.8 %copy-start.76 = (f32[4,1,128]{2,1,0:T(1,128)S(1)}, f32[4,1,128]{2,1,0:T(1,128)}, u32[]{:S(2)}) copy-start(f32[4,1,128]{2,1,0:T(1,128)} %param.6) | copy-start | bytes 6148
  384.9 13.8 %copy-start.19 = (f32[8,16,8,129]{3,2,1,0:T(8,128)S(1)}, f32[8,16,8,129]{3,2,1,0:T(8,128)}, u32[]{:S(2)}) copy-start(f32[8,16,8,129]{3,2,1,0:T(8,128)} %fusion.14) | copy-start | bytes 1585156
  386.4 5.5 collective-permute-start.10
  387.7 5.0 collective-permute-start.11
  392.9 92.2 %copy-start.67 = (s32[16384]{0:T(1024)S(1)}, s32[16384]{0:T(1024)}, u32[]{:S(2)}) copy-start(s32[16384]{0:T(1024)} %get-tuple-element.66) | copy-start | bytes 196612
  392.9 6.1 collective-permute-start.13
  394.3 5.1 collective-permute-start.12
  399.5 4.4 collective-permute-start.14
  400.8 3.9 collective-permute-start.15
  404.9 12.9 %collective-permute-start.17 = (f32[1,128]{1,0:T(1,128)S(1)}, f32[1,128]{1,0:T(1,128)S(1)}, u32[]{:S(2)}, u32[]{:S(2)}) collective-permute-start(f32[1,128]{1,0:T(1,128)S(1)} %fusion.177), channel_id=1, source_target_pairs={{2,0},{4,2},{6,4},{8,6},{10,8},{12,10},{14,12},{16,14},{18,16},{20... | collective-permute-start | bytes 1544 | tf_op jit(solution)/shard_map/ppermute | solution.py:24
  406.2 11.6 %collective-permute-start.16 = (f32[1,128]{1,0:T(1,128)S(1)}, f32[1,128]{1,0:T(1,128)S(1)}, u32[]{:S(2)}, u32[]{:S(2)}) collective-permute-start(f32[1,128]{1,0:T(1,128)S(1)} %fusion.177), channel_id=1, source_target_pairs={{0,2},{2,4},{4,6},{6,8},{8,10},{10,12},{12,14},{14,16},{16,18},{18... | collective-permute-start | bytes 1544 | tf_op jit(solution)/shard_map/ppermute | solution.py:21
  410.9 234.8 %collective-permute-start.4 = (f32[8,16,2,128]{3,2,1,0:T(2,128)S(1)}, f32[8,16,2,128]{3,2,1,0:T(2,128)S(1)}, u32[]{:S(2)}, u32[]{:S(2)}) collective-permute-start(f32[8,16,2,128]{3,2,1,0:T(2,128)S(1)} %get-tuple-element.176), channel_id=1, source_target_pairs={{0,2},{2,4},{4,6},{6,8},{8,10},{10,12},{12,14},{14,16},{16,18},{18... | collective-permute-start | bytes 393224 | tf_op jit(solution)/shard_map/ppermute | solution.py:21
  412.7 233.0 %collective-permute-start.5 = (f32[8,16,2,128]{3,2,1,0:T(2,128)S(1)}, f32[8,16,2,128]{3,2,1,0:T(2,128)S(1)}, u32[]{:S(2)}, u32[]{:S(2)}) collective-permute-start(f32[8,16,2,128]{3,2,1,0:T(2,128)S(1)} %get-tuple-element.177), channel_id=1, source_target_pairs={{2,0},{4,2},{6,4},{8,6},{10,8},{12,10},{14,12},{16,14},{18,16},{20... | collective-permute-start | bytes 393224 | tf_op jit(solution)/shard_map/ppermute | solution.py:24
  417.9 4.4 collective-permute-start.18
  419.2 3.9 collective-permute-start.19
  423.4 222.4 %copy-start.75 = (f32[1,128]{1,0:T(1,128)}, f32[1,128]{1,0:T(1,128)S(1)}, u32[]{:S(2)}) copy-start(f32[1,128]{1,0:T(1,128)S(1)} %fusion.175) | copy-start | bytes 1540
  645.8 1.4 collective-permute-start.6
  646.0 1.5 collective-permute-start.7
  654.5 4.1 copy-start.5
  654.6 4.1 copy-start.7
  654.6 4.1 copy-start.29
  654.6 4.1 copy-start.31
  (50 other events, 63.4 us)
Sparse Core Ops, SparseCore 0:
  136.1 241.9 all-reduce.2
where the time goes:
time: 685 us; the launch traced here: 684 us
  waiting for transfers between devices  233 us (34%)
  local copies, waits for them, and re-layouts  191 us (28%)
  other arithmetic  131 us (19%)
  blocking collectives  61.8 us (9%)
  starting transfers between devices  51.8 us (8%)
  between operations  15.3 us (2%)
    unnamed x2, waiting for transfers between devices  228 us
    gather x1, local copies, waits for them, and re-layouts, body(): footpoint_potential = whole_table[node_slot]  161 us
    scatter-add x1, other arithmetic, body(): jax.ops.segment_sum(cell_current, node_slot.reshape(-1), num_segments=NLA...  86.9 us
    all_gather x1, blocking collectives, body(): lax.all_gather(potential.reshape(-1), ('shell', 'radial'), axis=0, tiled=...  61.8 us
    ppermute x10, starting transfers between devices, padded_2(): lax.ppermute(lax.slice_in_dim(block, 0, width, axis=dim), axis, backward)  28.9 us
    ppermute x10, starting transfers between devices, padded_2(): lax.ppermute(lax.slice_in_dim(block, block.shape[dim] - width, None, axis...  22.8 us
  transfers between devices with their start and end apart: 21, of which 9 were waited for; matrix products, arithmetic and copies ran while one was open for 26% of the time, Pallas kernels for 0%

commit v1 on v0

--- a/solution.py
+++ b/solution.py
@@ -169,7 +169,9 @@
         coupled = coupled + conductance[2] * padded_panel[1:-1, :-2]
         coupled = coupled + conductance[3] * padded_panel[1:-1, 2:]
         potential = apply_blocks(coupled)
-    whole_table = lax.all_gather(potential.reshape(-1), ("shell", "radial"), axis=0, tiled=True)
+    block_2 = potential.reshape(-1)
+    outgoing = jnp.stack([block_2] * lax.axis_size(("shell", "radial")))
+    whole_table = jnp.concatenate(lax.all_to_all(outgoing, ("shell", "radial"), 0, 0), axis=0)
     footpoint_potential = whole_table[node_slot]
     return (state_next, potential, footpoint_potential)
 

time: 685 us -> 639 us (0.933)
  blocking collectives: 61.8 us -> 0 us
  starting transfers between devices: 51.8 us -> 67.3 us
    all_gather x1 -> x0, blocking collectives: 61.8 us -> none  [body(): lax.all_gather(potential.reshape(-1), ('shell', 'radial'), axis=0, tiled=...]
    all_to_all x0 -> x1, starting transfers between devices: none -> 13.6 us  [body(): lax.all_to_all(outgoing, ('shell', 'radial'), 0, 0)]
  transfers between devices with their start and end apart: 21 -> 22, of which waited for: 9 -> 9; matrix products, arithmetic and copies ran while one was open for 26% -> 7% of each run, Pallas kernels for 0% -> 0%
where the time goes in v1:
time: 639 us; the launch traced here: 638 us
  waiting for transfers between devices  233 us (36%)
  local copies, waits for them, and re-layouts  191 us (30%)
  other arithmetic  130 us (20%)
  starting transfers between devices  67.3 us (11%)
  between operations  15.4 us (2%)
    unnamed x2, waiting for transfers between devices  228 us
    gather x1, local copies, waits for them, and re-layouts, body(): footpoint_potential = whole_table[node_slot]  161 us
    scatter-add x1, other arithmetic, body(): jax.ops.segment_sum(cell_current, node_slot.reshape(-1), num_segments=NLA...  86.9 us
    ppermute x10, starting transfers between devices, padded_2(): lax.ppermute(lax.slice_in_dim(block, 0, width, axis=dim), axis, backward)  28.8 us
    ppermute x10, starting transfers between devices, padded_2(): lax.ppermute(lax.slice_in_dim(block, block.shape[dim] - width, None, axis...  24.9 us
    slice x6, local copies, waits for them, and re-layouts, pad_latitude(): return jnp.pad(field, ((0, 0), (0, 0), (0, 0), (2, 2)), mode='edge')  13.6 us
    all_to_all x1, starting transfers between devices, body(): lax.all_to_all(outgoing, ('shell', 'radial'), 0, 0)  13.6 us
  transfers between devices with their start and end apart: 22, of which 9 were waited for; matrix products, arithmetic and copies ran while one was open for 7% of the time, Pallas kernels for 0%

profile of v1, /device:TPU:1, one launch (start us, length us, event | category | flops | bytes accessed | tf_op | source)
XLA Modules:
  0.0 637.9 jit_solution(11354747382657837081)
XLA Ops:
  7.2 1.4 fusion.271
  8.6 2.5 collective-permute-start
  11.1 8.7 %collective-permute-start.1 = (f32[8,16,2,128]{3,2,1,0:T(2,128)S(1)}, f32[8,16,2,128]{3,2,1,0:T(2,128)S(1)}, u32[]{:S(2)}, u32[]{:S(2)}) collective-permute-start(f32[8,16,2,128]{3,2,1,0:T(2,128)S(1)} %get-tuple-element.179), channel_id=1, source_target_pairs={{2,0},{4,2},{6,4},{8,6},{10,8},{12,10},{14,12},{16,14},{18,16},{20... | collective-permute-start | bytes 393224 | tf_op jit(solution)/shard_map/ppermute | solution.py:24
  20.9 1.6 fusion.158
  23.0 0.9 pad_maximum_fusion.19
  24.0 1.2 collective-permute-start.2
  26.9 0.9 slice_subtract_fusion.4
  27.8 1.1 slice_subtract_fusion.2
  28.9 1.6 fusion.269
  30.5 2.5 copy.843
  33.0 1.2 copy.844
  36.1 2.6 pad_maximum_fusion
  39.9 1.5 multiply_reduce_fusion.31
  42.6 1.8 multiply_reduce_fusion.22
  45.1 1.6 multiply_reduce_fusion.19
  49.2 86.9 %scatter_custom_fusion = f32[32768]{0:T(1024)} fusion(s32[16384]{0:T(1024)} %bitcast.616, f32[16384]{0:T(1024)} %bitcast.617, f32[]{:T(128)} %constant.97.clone.1), kind=kCustom, calls=%fused_computation.431 | custom fusion | flops 16384 | bytes 131584 | tf_op jit(solution)/shard_map/scatter-add | solution.py:153
  136.1 2.6 slice_subtract_fusion.1
  147.7 1.3 fusion.14
  149.0 0.9 multiply_add_fusion.10
  149.9 228.2 %all-reduce.3.cloned.1.call-done = f32[32768]{0:T(1024)} async-done(((f32[32768]{0:T(1024)}), f32[32768]{0:T(1024)}) %all-reduce.3.cloned.1.call-update) | async-done | bytes 131088
  379.1 1.3 collective-permute-start.9
  380.4 4.4 collective-permute-start.8
  384.9 1.4 fusion.24
  386.4 1.3 collective-permute-start.10
  387.7 4.2 collective-permute-start.11
  392.9 1.3 collective-permute-start.13
  394.2 4.3 collective-permute-start.12
  399.3 1.3 collective-permute-start.14
  400.6 3.1 collective-permute-start.15
  404.8 1.3 collective-permute-start.17
  406.1 4.5 collective-permute-start.16
  410.7 1.8 collective-permute-start.4
  412.6 5.2 collective-permute-start.5
  417.8 1.3 collective-permute-start.18
  419.1 3.1 collective-permute-start.19
  424.0 13.6 %all-to-all-start = ((f32[256,1,128]{2,1,0:T(1,128)}), f32[256,1,128]{2,1,0:T(1,128)S(1)}, u32[]{:S(2)}, u32[]{:S(2)}) async-start(f32[256,1,128]{2,1,0:T(1,128)} %stack.3), calls=%async_computation | async-start | bytes 262144 | tf_op jit(solution)/shard_map/all_to_all | solution.py:174
  437.6 2.2 collective-permute-start.6
  441.8 1.9 fusion.268
  444.2 1.6 multiply_reduce_fusion.28
  445.8 1.4 multiply_reduce_fusion.25
  448.4 1.0 multiply_reduce_fusion.10
  450.1 1.6 multiply_reduce_fusion.7
  452.4 3.2 copy.860
  455.5 3.2 copy.861
  458.7 1.3 reshape.273
  460.4 1.0 fusion.4
  469.3 1.1 fusion.32
  470.4 160.6 %gather_fusion = f32[16384]{0:T(1024)} fusion(f32[32768]{0:T(1024)S(1)} %bitcast.596, s32[16384]{0:T(1024)S(1)} %copy-done.68), kind=kCustom, calls=%fused_computation | custom fusion | bytes 196608 | tf_op jit(solution)/shard_map/gather | solution.py:175
  (280 shorter events, 37.8 us)
Async XLA Ops:
  7.2 371.8 %copy-start = (f32[1,1,128,128]{3,2,1,0:T(8,128)S(1)}, f32[1,1,128,128]{3,2,1,0:T(8,128)}, u32[]{:S(2)}) copy-start(f32[1,1,128,128]{3,2,1,0:T(8,128)} %param.7) | copy-start | bytes 196612
  7.2 18.3 %copy-start.4 = (f32[8,16,8,128]{3,2,1,0:T(8,128)S(1)}, f32[8,16,8,128]{3,2,1,0:T(8,128)}, u32[]{:S(2)}) copy-start(f32[8,16,8,128]{3,2,1,0:T(8,128)} %param.4) | copy-start | bytes 1572868
  7.2 371.0 %all-reduce.3.cloned.1.call-start = ((), (), s32[]{:S(2)}) async-start(), calls=%async_computation.1 | async-start | bytes 262144
  8.6 14.4 %collective-permute-start = (f32[8,16,2,128]{3,2,1,0:T(2,128)S(1)}, f32[8,16,2,128]{3,2,1,0:T(2,128)S(1)}, u32[]{:S(2)}, u32[]{:S(2)}) collective-permute-start(f32[8,16,2,128]{3,2,1,0:T(2,128)S(1)} %get-tuple-element.178), channel_id=1, source_target_pairs={{0,2},{2,4},{4,6},{6,8},{8,10},{10,12},{12,14},{14,16},{16,18},{18... | collective-permute-start | bytes 393224 | tf_op jit(solution)/shard_map/ppermute | solution.py:21
  11.1 11.9 %collective-permute-start.1 = (f32[8,16,2,128]{3,2,1,0:T(2,128)S(1)}, f32[8,16,2,128]{3,2,1,0:T(2,128)S(1)}, u32[]{:S(2)}, u32[]{:S(2)}) collective-permute-start(f32[8,16,2,128]{3,2,1,0:T(2,128)S(1)} %get-tuple-element.179), channel_id=1, source_target_pairs={{2,0},{4,2},{6,4},{8,6},{10,8},{12,10},{14,12},{16,14},{18,16},{20... | collective-permute-start | bytes 393224 | tf_op jit(solution)/shard_map/ppermute | solution.py:24
  23.0 3.9 copy-start.69
  24.0 2.2 collective-permute-start.2
  25.2 1.3 collective-permute-start.3
  42.5 4.2 copy-start.9
  42.5 4.1 copy-start.11
  42.6 4.1 copy-start.28
  141.0 3.2 copy-start.23
  141.0 3.2 copy-start.35
  141.0 3.2 copy-start.51
  141.0 3.2 copy-start.53
  141.2 3.1 copy-start.10
  141.2 3.1 copy-start.12
  141.2 3.1 copy-start.22
  141.2 3.1 copy-start.34
  149.0 235.9 %copy-start.59 = (f32[17,8,128]{2,1,0:T(8,128)S(1)}, f32[17,8,128]{2,1,0:T(8,128)}, u32[]{:S(2)}) copy-start(f32[17,8,128]{2,1,0:T(8,128)} %get-tuple-element.83) | copy-start | bytes 208900
  379.1 7.2 %collective-permute-start.9 = (f32[1,128]{1,0:T(1,128)S(1)}, f32[1,128]{1,0:T(1,128)S(1)}, u32[]{:S(2)}, u32[]{:S(2)}) collective-permute-start(f32[1,128]{1,0:T(1,128)S(1)} %fusion.181), channel_id=1, source_target_pairs={{2,0},{4,2},{6,4},{8,6},{10,8},{12,10},{14,12},{16,14},{18,16},{20... | collective-permute-start | bytes 1544 | tf_op jit(solution)/shard_map/ppermute | solution.py:24
  380.4 5.9 collective-permute-start.8
  384.9 7.8 %copy-start.77 = (f32[4,1,128]{2,1,0:T(1,128)S(1)}, f32[4,1,128]{2,1,0:T(1,128)}, u32[]{:S(2)}) copy-start(f32[4,1,128]{2,1,0:T(1,128)} %param.6) | copy-start | bytes 6148
  384.9 13.7 %copy-start.21 = (f32[8,16,8,129]{3,2,1,0:T(8,128)S(1)}, f32[8,16,8,129]{3,2,1,0:T(8,128)}, u32[]{:S(2)}) copy-start(f32[8,16,8,129]{3,2,1,0:T(8,128)} %fusion.14) | copy-start | bytes 1585156
  386.4 5.5 collective-permute-start.10
  387.7 5.0 collective-permute-start.11
  392.9 6.0 collective-permute-start.13
  394.2 5.1 collective-permute-start.12
  399.3 4.4 collective-permute-start.14
  400.6 3.9 collective-permute-start.15
  404.8 13.0 %collective-permute-start.17 = (f32[1,128]{1,0:T(1,128)S(1)}, f32[1,128]{1,0:T(1,128)S(1)}, u32[]{:S(2)}, u32[]{:S(2)}) collective-permute-start(f32[1,128]{1,0:T(1,128)S(1)} %fusion.177), channel_id=1, source_target_pairs={{2,0},{4,2},{6,4},{8,6},{10,8},{12,10},{14,12},{16,14},{18,16},{20... | collective-permute-start | bytes 1544 | tf_op jit(solution)/shard_map/ppermute | solution.py:24
  406.1 11.6 %collective-permute-start.16 = (f32[1,128]{1,0:T(1,128)S(1)}, f32[1,128]{1,0:T(1,128)S(1)}, u32[]{:S(2)}, u32[]{:S(2)}) collective-permute-start(f32[1,128]{1,0:T(1,128)S(1)} %fusion.177), channel_id=1, source_target_pairs={{0,2},{2,4},{4,6},{6,8},{8,10},{10,12},{12,14},{14,16},{16,18},{18... | collective-permute-start | bytes 1544 | tf_op jit(solution)/shard_map/ppermute | solution.py:21
  410.7 30.5 %copy-start.70 = (pred[20]{0:T(512)(128)(4,1)S(1)}, pred[20]{0:T(512)(128)(4,1)}, u32[]{:S(2)}) copy-start(pred[20]{0:T(512)(128)(4,1)} %copy-done.69) | copy-start | bytes 64
  410.7 26.8 %collective-permute-start.4 = (f32[8,16,2,128]{3,2,1,0:T(2,128)S(1)}, f32[8,16,2,128]{3,2,1,0:T(2,128)S(1)}, u32[]{:S(2)}, u32[]{:S(2)}) collective-permute-start(f32[8,16,2,128]{3,2,1,0:T(2,128)S(1)} %get-tuple-element.176), channel_id=1, source_target_pairs={{0,2},{2,4},{4,6},{6,8},{8,10},{10,12},{12,14},{14,16},{16,18},{18... | collective-permute-start | bytes 393224 | tf_op jit(solution)/shard_map/ppermute | solution.py:21
  412.6 25.0 %collective-permute-start.5 = (f32[8,16,2,128]{3,2,1,0:T(2,128)S(1)}, f32[8,16,2,128]{3,2,1,0:T(2,128)S(1)}, u32[]{:S(2)}, u32[]{:S(2)}) collective-permute-start(f32[8,16,2,128]{3,2,1,0:T(2,128)S(1)} %get-tuple-element.177), channel_id=1, source_target_pairs={{2,0},{4,2},{6,4},{8,6},{10,8},{12,10},{14,12},{16,14},{18,16},{20... | collective-permute-start | bytes 393224 | tf_op jit(solution)/shard_map/ppermute | solution.py:24
  417.8 4.4 collective-permute-start.18
  419.1 3.9 collective-permute-start.19
  423.2 18.4 %copy-start.76 = (f32[1,128]{1,0:T(1,128)}, f32[1,128]{1,0:T(1,128)S(1)}, u32[]{:S(2)}) copy-start(f32[1,128]{1,0:T(1,128)S(1)} %fusion.175) | copy-start | bytes 1540
  424.0 46.4 %all-to-all-start = ((f32[256,1,128]{2,1,0:T(1,128)}), f32[256,1,128]{2,1,0:T(1,128)S(1)}, u32[]{:S(2)}, u32[]{:S(2)}) async-start(f32[256,1,128]{2,1,0:T(1,128)} %stack.3), calls=%async_computation | async-start | bytes 262144 | tf_op jit(solution)/shard_map/all_to_all | solution.py:174
  437.6 3.2 collective-permute-start.6
  439.9 1.3 collective-permute-start.7
  444.1 3.1 copy-start.18
  444.2 3.1 copy-start.46
  448.4 3.4 copy-start.5
  448.4 3.4 copy-start.7
  448.4 3.3 copy-start.30
  448.4 3.3 copy-start.32
  470.4 160.6 %copy-start.1 = (f32[1,1,128,128]{3,2,1,0:T(8,128)S(1)}, f32[1,1,128,128]{3,2,1,0:T(8,128)}, u32[]{:S(2)}) copy-start(f32[1,1,128,128]{3,2,1,0:T(8,128)} %param.7) | copy-start | bytes 196612
  (52 other events, 71.4 us)
Sparse Core Ops, SparseCore 0:
  136.2 241.9 all-reduce.2
